TPU v7x, 512 devices: a whole 4x4x16 slice. The times are simulated.
512 devices in a mesh: dp: 8 (over y, x_lo), ctx: 64 (over z, x_hi, core).
Axes of the slice: x: 4 (x_hi: 2, x_lo: 2; x = x_hi * 2 + x_lo), y: 4, z: 16, core: 2. Of those that a mesh axis runs over, the one named last changes fastest.
Arguments:
- events: bfloat16 [8, 16384, 1024], P('dp', 'ctx'), may hold values from -6 to 6
- w_query: bfloat16 [1024, 512], replicated, may hold values from -0.1875 to 0.1875
- w_key: bfloat16 [1024, 512], replicated, may hold values from -0.1875 to 0.1875
- values: bfloat16 [8, 16384, 512], P('dp', 'ctx'), may hold values from -6 to 6
- grad_out: bfloat16 [8, 16384, 512], P('dp', 'ctx'), may hold values from -6 to 6
- lengths: int32 [8, 32], P('dp'), may hold values from 1 to 768, 16384 in all within a row
- stream_shift: int32 [8], P('dp'), may hold values from 0 to 16383
- block_keep: int32 [8, 128], P('dp'), may hold values 0 or 1
Outputs:
- attended: bfloat16 [8, 16384, 512], P('dp', 'ctx')
- grad_values: bfloat16 [8, 16384, 512], P('dp', 'ctx')
- grad_wq: bfloat16 [1024, 512], P('ctx')
- grad_wk: bfloat16 [1024, 512], P('ctx')
Inputs may be any that keep to these rules, and one draw needn't show every extreme that they name: The lengths of a stream sum to 16384; the longest is exactly 768.
All inputs are finite; a program needn't handle non-finite values. No bound on the sum of `block_keep` on one device may be relied on, other than what follows from the above.
Results may differ from a plain program's by a relative error of at most 0.011.
Values may be sent and summed in bfloat16 or wider, within the bound.
A program may use at most 64 MiB of HBM per device.

v0:
```python
import jax
import jax.numpy as jnp
from jax import lax
from jax.sharding import PartitionSpec as P

HD = 128
SPAN = 3
BLOCK = 128
MAXLEN = 768


def from_behind(value, axis, steps):
    count = lax.axis_size(axis)
    pairs = [(source, (source + steps) % count) for source in range(count)]
    return lax.ppermute(value, axis, pairs)


def tile_terms(query, grad, key, value, valid, scale, alpha):
    z = jnp.einsum("qhd,khd->hqk", query, key, preferred_element_type=jnp.float32) * alpha
    sig = jax.nn.sigmoid(z)
    weight = valid[None, :, :].astype(jnp.float32) * scale
    att = (z * sig * weight).astype(jnp.bfloat16)
    out = jnp.einsum("hqk,khd->qhd", att, value, preferred_element_type=jnp.float32)
    dprod = jnp.einsum("qhd,khd->hqk", grad, value, preferred_element_type=jnp.float32)
    dsc = (dprod * sig * (1.0 + z * (1.0 - sig)) * weight * alpha).astype(jnp.bfloat16)
    dquery = jnp.einsum("hqk,khd->qhd", dsc, key, preferred_element_type=jnp.float32)
    dkey = jnp.einsum("hqk,qhd->khd", dsc, query, preferred_element_type=jnp.float32)
    dvalue = jnp.einsum("hqk,qhd->khd", att, grad, preferred_element_type=jnp.float32)
    return (out, dquery, dkey, dvalue)


def body(events, w_query, w_key, values, grad_out, lengths, stream_shift, block_keep):
    rows = events.shape[1]
    features = w_query.shape[1]
    nheads = features // HD
    alpha = 1.0 / HD**0.5
    scale = 1.0 / MAXLEN**0.5
    local = events[0]
    queries = jnp.dot(local, w_query, preferred_element_type=jnp.float32).astype(jnp.bfloat16)
    keys = jnp.dot(local, w_key, preferred_element_type=jnp.float32).astype(jnp.bfloat16)
    queries = queries.reshape(rows, nheads, HD)
    keys = keys.reshape(rows, nheads, HD)
    vals = values[0].reshape(rows, nheads, HD)
    cotan = grad_out[0].reshape(rows, nheads, HD)
    cycle_size = lax.axis_size("ctx")
    myself = lax.axis_index("ctx")
    total = rows * cycle_size
    ends = jnp.cumsum(lengths[0])
    offset = stream_shift[0]
    keep = block_keep[0]
    blocks_all = jnp.arange(keep.shape[0], dtype=jnp.int32)
    within = jnp.arange(rows, dtype=jnp.int32)

    def describe(anchor):
        anchor = jnp.remainder(anchor, cycle_size)
        position = jnp.remainder(anchor * rows + within - offset, total)
        owner = jnp.sum((position[:, None] >= ends[None, :]).astype(jnp.int32), axis=1)
        which = position // BLOCK
        kept = (
            jnp.sum(jnp.where(which[:, None] == blocks_all[None, :], keep[None, :], 0), axis=1) > 0
        )
        return (position, owner, kept)

    zeros = jnp.zeros((rows, nheads, HD), jnp.float32)
    qinfo = describe(myself)
    moving = (keys, vals)
    carried = (zeros, zeros)
    out_acc = zeros
    dq_acc = zeros
    for step in range(SPAN + 1):
        if step > 0:
            moving = from_behind((moving[0], moving[1]), "ctx", 1)
            carried = (
                from_behind(carried[0].astype(jnp.bfloat16), "ctx", 1).astype(jnp.float32),
                from_behind(carried[1].astype(jnp.bfloat16), "ctx", 1).astype(jnp.float32),
            )
        kinfo = describe(myself - step)
        o, a, b, c = tile_terms(
            queries,
            cotan,
            moving[0],
            moving[1],
            (qinfo[1][:, None] == kinfo[1][None, :])
            & (kinfo[0][None, :] <= qinfo[0][:, None])
            & kinfo[2][None, :],
            scale,
            alpha,
        )
        out_acc = out_acc + o
        dq_acc = dq_acc + a
        carried = (carried[0] + b, carried[1] + c)
    carried = (
        from_behind(carried[0].astype(jnp.bfloat16), "ctx", -SPAN).astype(jnp.float32),
        from_behind(carried[1].astype(jnp.bfloat16), "ctx", -SPAN).astype(jnp.float32),
    )
    dk_acc, dv_acc = carried
    attended = out_acc.reshape(1, rows, features).astype(jnp.bfloat16)
    grad_values = dv_acc.reshape(1, rows, features).astype(jnp.bfloat16)
    dq_b = dq_acc.reshape(rows, features).astype(jnp.bfloat16)
    dk_b = dk_acc.reshape(rows, features).astype(jnp.bfloat16)
    joined = jnp.concatenate([dq_b, dk_b], axis=1)
    width_rows = local.shape[1]
    share = width_rows // cycle_size
    terms = jnp.einsum("rd,rf->df", local, joined, preferred_element_type=jnp.float32)
    summed = lax.psum(terms, ("dp", "ctx"))
    mine = lax.dynamic_slice_in_dim(summed, myself * share, share, 0)
    grad_wq = mine[:, :features].astype(jnp.bfloat16)
    grad_wk = mine[:, features:].astype(jnp.bfloat16)
    return (attended, grad_values, grad_wq, grad_wk)


def solution(mesh):
    placed = (
        P("dp", "ctx", None),
        P(),
        P(),
        P("dp", "ctx", None),
        P("dp", "ctx", None),
        P("dp", None),
        P("dp"),
        P("dp", None),
    )
    return jax.shard_map(
        body,
        mesh=mesh,
        in_specs=placed,
        out_specs=(P("dp", "ctx", None), P("dp", "ctx", None), P("ctx", None), P("ctx", None)),
        check_vma=False,
    )
```

profile of v0, /device:TPU:7, one launch (start us, length us, event | category | flops | bytes accessed | tf_op | source)
XLA Modules:
  0.0 291.1 jit_solution(15227647348382941098)
XLA Ops:
  0.6 1.2 copy.87
  1.8 4.9 %collective-permute-start.1 = (bf16[256,4,128]{0,2,1:T(8,128)(2,1)S(1)}, bf16[256,4,128]{0,2,1:T(8,128)(2,1)S(1)}, u32[]{:S(2)}, u32[]{:S(2)}) collective-permute-start(bf16[256,4,128]{0,2,1:T(8,128)(2,1)S(1)} %bitcast.101), channel_id=1, source_target_pairs={{0,1},{1,2},{2,3},{3,4},{4,5},{5,6},{6,7},{7,8},{8,9},{9,10},{10,1... | collective-permute-start | bytes 786440 | tf_op jit(solution)/shard_map/ppermute | solution.py:15
  6.8 1.5 fusion.20
  8.3 0.7 copy.157
  9.0 1.9 collective-permute-start
  11.7 1.0 select_reduce_fusion
  12.8 0.7 copy.86
  13.6 0.1 reduce
  13.7 1.0 reshape_squeeze.7
  14.8 1.8 convolution_convert_fusion.3
  16.6 0.1 copy.132
  16.7 0.1 convert_reduce_fusion
  16.8 1.2 and_select_fusion
  18.0 0.5 multiply_convert_fusion.3
  18.6 0.5 fusion.15
  19.1 1.0 fusion.19
  20.1 4.1 %collective-permute-start.10 = (bf16[256,4,128]{0,2,1:T(8,128)(2,1)}, bf16[256,4,128]{0,2,1:T(8,128)(2,1)}, u32[]{:S(2)}, u32[]{:S(2)}) collective-permute-start(bf16[256,4,128]{0,2,1:T(8,128)(2,1)} %fusion.19), channel_id=1, source_target_pairs={{0,1},{1,2},{2,3},{3,4},{4,5},{5,6},{6,7},{7,8},{8,9},{9,10},{10,1... | collective-permute-start | bytes 786440 | tf_op jit(solution)/shard_map/ppermute | solution.py:15
  24.2 1.1 fusion.18
  25.3 1.9 collective-permute-start.6
  27.2 0.3 fusion.44
  27.5 0.3 fusion.42
  27.8 1.6 multiply_convert_fusion.2
  29.4 0.5 fusion.14
  30.0 1.2 add_convert_fusion.2
  31.2 4.8 %collective-permute-start.11 = (bf16[256,4,128]{0,2,1:T(8,128)(2,1)S(1)}, bf16[256,4,128]{0,2,1:T(8,128)(2,1)S(1)}, u32[]{:S(2)}, u32[]{:S(2)}) collective-permute-start(bf16[256,4,128]{0,2,1:T(8,128)(2,1)S(1)} %add_convert_fusion.2), channel_id=1, source_target_pairs={{0,1},{1,2},{2,3},{3,4},{4,5},{5,6},{6,7},{7,8},{8,9},{9,10},{10,1... | collective-permute-start | bytes 786440 | tf_op jit(solution)/shard_map/ppermute | solution.py:15
  36.0 1.3 add_convert_fusion.5
  37.3 1.9 collective-permute-start.7
  39.2 4.1 %collective-permute-start.3 = (bf16[256,4,128]{0,2,1:T(8,128)(2,1)S(1)}, bf16[256,4,128]{0,2,1:T(8,128)(2,1)S(1)}, u32[]{:S(2)}, u32[]{:S(2)}) collective-permute-start(bf16[256,4,128]{0,2,1:T(8,128)(2,1)S(1)} %collective-permute-done.1), channel_id=1, source_target_pairs={{0,1},{1,2},{2,3},{3,4},{4,5},{5,6},{6,7},{7,8},{8,9},{9,10},{10,1... | collective-permute-start | bytes 786440 | tf_op jit(solution)/shard_map/ppermute | solution.py:15
  43.4 1.9 collective-permute-start.2
  45.3 0.3 convolution_add_fusion.5
  45.6 1.3 convolution_add_fusion.2
  46.9 2.7 collective-permute-done.2
  49.6 0.5 multiply_convert_fusion.1
  50.2 0.5 fusion.13
  50.7 0.2 convolution_bitcast_fusion.2
  51.0 6.7 %collective-permute-start.12 = (bf16[256,4,128]{0,2,1:T(8,128)(2,1)S(1)}, bf16[256,4,128]{0,2,1:T(8,128)(2,1)S(1)}, u32[]{:S(2)}, u32[]{:S(2)}) collective-permute-start(bf16[256,4,128]{0,2,1:T(8,128)(2,1)S(1)} %add_convert_fusion.1), channel_id=1, source_target_pairs={{0,1},{1,2},{2,3},{3,4},{4,5},{5,6},{6,7},{7,8},{8,9},{9,10},{10,1... | collective-permute-start | bytes 786440 | tf_op jit(solution)/shard_map/ppermute | solution.py:15
  57.7 0.3 convolution_bitcast_fusion.5
  58.1 0.7 add_convert_fusion.4
  58.8 1.9 collective-permute-start.8
  60.7 3.9 %collective-permute-start.5 = (bf16[256,4,128]{0,2,1:T(8,128)(2,1)S(1)}, bf16[256,4,128]{0,2,1:T(8,128)(2,1)S(1)}, u32[]{:S(2)}, u32[]{:S(2)}) collective-permute-start(bf16[256,4,128]{0,2,1:T(8,128)(2,1)S(1)} %collective-permute-done.3), channel_id=1, source_target_pairs={{0,1},{1,2},{2,3},{3,4},{4,5},{5,6},{6,7},{7,8},{8,9},{9,10},{10,1... | collective-permute-start | bytes 786440 | tf_op jit(solution)/shard_map/ppermute | solution.py:15
  64.6 1.9 collective-permute-start.4
  66.5 0.3 convolution_add_fusion.4
  66.9 0.3 convolution_add_fusion.1
  67.2 3.5 %collective-permute-done.4 = bf16[256,4,128]{2,0,1:T(8,128)(2,1)S(1)} collective-permute-done((bf16[256,4,128]{2,0,1:T(8,128)(2,1)S(1)}, bf16[256,4,128]{2,0,1:T(8,128)(2,1)S(1)}, u32[]{:S(2)}, u32[]{:S(2)}) %collective-permute-start.4) | collective-permute-done | bytes 262176 | tf_op jit(solution)/shard_map/ppermute | solution.py:15
  70.7 0.5 multiply_convert_fusion
  71.3 0.1 copy-done.5
  71.4 0.5 fusion.12
  72.0 0.2 convolution_bitcast_fusion.1
  72.2 1.0 fusion.16
  73.2 0.8 add_convert_fusion
  74.0 1.8 copy.117
  75.8 9.6 %collective-permute-start.13 = (bf16[256,4,128]{0,2,1:T(8,128)(2,1)}, bf16[256,4,128]{0,2,1:T(8,128)(2,1)}, u32[]{:S(2)}, u32[]{:S(2)}) collective-permute-start(bf16[256,4,128]{0,2,1:T(8,128)(2,1)} %add_convert_fusion), channel_id=1, source_target_pairs={{0,61},{1,62},{2,63},{3,0},{4,1},{5,2},{6,3},{7,4},{8,5},{9,6},{10... | collective-permute-start | bytes 786440 | tf_op jit(solution)/shard_map/ppermute | solution.py:15
  85.4 0.3 convolution_bitcast_fusion.4
  85.8 1.0 add_convert_fusion.3
  86.8 2.1 collective-permute-start.9
  88.9 1.3 fusion.17
  90.2 4.3 %collective-permute-done.9 = bf16[256,4,128]{2,0,1:T(8,128)(2,1)S(1)} collective-permute-done((bf16[256,4,128]{2,0,1:T(8,128)(2,1)S(1)}, bf16[256,4,128]{2,0,1:T(8,128)(2,1)S(1)}, u32[]{:S(2)}, u32[]{:S(2)}) %collective-permute-start.9) | collective-permute-done | bytes 262176 | tf_op jit(solution)/shard_map/ppermute | solution.py:15
  94.5 0.1 copy.100
  94.6 0.8 copy.118
  95.5 3.6 %convolution_bitcast_fusion = f32[1024,1024]{0,1:T(8,128)} fusion(bf16[256,512]{0,1:T(8,128)(2,1)} %bitcast.18, bf16[256,512]{0,1:T(8,128)(2,1)S(1)} %bitcast.104, bf16[1,256,1024]{2,1,0:T(8,128)(2,1)S(1)} %copy-done.1), kind=kOutput, calls=%fused_computation | convolution fusion | flops 537919488 | bytes 5242880 | tf_op jit(solution)/shard_map/rd,rf->df/dot_general | solution.py:104
  99.1 190.5 %all-reduce.1 = bf16[1024,1024]{0,1:T(8,128)(2,1)S(1)} all-reduce(f32[1024,1024]{0,1:T(8,128)} %convolution_bitcast_fusion), channel_id=1, replica_groups=mesh['dp'=8,'ctx'=64] {'dp','ctx'}, use_global_device_ids=true, to_apply=%region_9.10 | all-reduce | flops 1048576 | bytes 6291456 | tf_op jit(solution)/shard_map/psum | solution.py:105
  289.6 0.2 dynamic-slice_convert_fusion
  289.8 0.7 copy.120
  290.5 0.7 copy.119
  (33 shorter events, 0.3 us)
Async XLA Ops:
  0.6 6.2 %copy-start = (bf16[1024,512]{1,0:T(8,128)(2,1)S(1)}, bf16[1024,512]{1,0:T(8,128)(2,1)}, u32[]{:S(2)}) copy-start(bf16[1024,512]{1,0:T(8,128)(2,1)} %param.10) | copy-start | bytes 3145732
  1.8 27.6 %collective-permute-start.1 = (bf16[256,4,128]{0,2,1:T(8,128)(2,1)S(1)}, bf16[256,4,128]{0,2,1:T(8,128)(2,1)S(1)}, u32[]{:S(2)}, u32[]{:S(2)}) collective-permute-start(bf16[256,4,128]{0,2,1:T(8,128)(2,1)S(1)} %bitcast.101), channel_id=1, source_target_pairs={{0,1},{1,2},{2,3},{3,4},{4,5},{5,6},{6,7},{7,8},{8,9},{9,10},{10,1... | collective-permute-start | bytes 786440 | tf_op jit(solution)/shard_map/ppermute | solution.py:15
  9.0 18.8 %collective-permute-start = (bf16[256,4,128]{2,0,1:T(8,128)(2,1)}, bf16[256,4,128]{2,0,1:T(8,128)(2,1)}, u32[]{:S(2)}, u32[]{:S(2)}) collective-permute-start(bf16[256,4,128]{2,0,1:T(8,128)(2,1)} %bitcast.88), channel_id=1, source_target_pairs={{0,1},{1,2},{2,3},{3,4},{4,5},{5,6},{6,7},{7,8},{8,9},{9,10},{10,1... | collective-permute-start | bytes 786440 | tf_op jit(solution)/shard_map/ppermute | solution.py:15
  20.1 9.9 %collective-permute-start.10 = (bf16[256,4,128]{0,2,1:T(8,128)(2,1)}, bf16[256,4,128]{0,2,1:T(8,128)(2,1)}, u32[]{:S(2)}, u32[]{:S(2)}) collective-permute-start(bf16[256,4,128]{0,2,1:T(8,128)(2,1)} %fusion.19), channel_id=1, source_target_pairs={{0,1},{1,2},{2,3},{3,4},{4,5},{5,6},{6,7},{7,8},{8,9},{9,10},{10,1... | collective-permute-start | bytes 786440 | tf_op jit(solution)/shard_map/ppermute | solution.py:15
  25.3 10.7 %collective-permute-start.6 = (bf16[256,4,128]{2,0,1:T(8,128)(2,1)}, bf16[256,4,128]{2,0,1:T(8,128)(2,1)}, u32[]{:S(2)}, u32[]{:S(2)}) collective-permute-start(bf16[256,4,128]{2,0,1:T(8,128)(2,1)} %fusion.18), channel_id=1, source_target_pairs={{0,1},{1,2},{2,3},{3,4},{4,5},{5,6},{6,7},{7,8},{8,9},{9,10},{10,1... | collective-permute-start | bytes 786440 | tf_op jit(solution)/shard_map/ppermute | solution.py:15
  27.5 1.9 copy-start.4
  30.0 19.6 %copy-start.3 = (f32[256,256]{1,0:T(8,128)S(1)}, f32[256,256]{1,0:T(8,128)}, u32[]{:S(2)}) copy-start(f32[256,256]{1,0:T(8,128)} %get-tuple-element.27) | copy-start | bytes 786436
  31.2 19.7 %collective-permute-start.11 = (bf16[256,4,128]{0,2,1:T(8,128)(2,1)S(1)}, bf16[256,4,128]{0,2,1:T(8,128)(2,1)S(1)}, u32[]{:S(2)}, u32[]{:S(2)}) collective-permute-start(bf16[256,4,128]{0,2,1:T(8,128)(2,1)S(1)} %add_convert_fusion.2), channel_id=1, source_target_pairs={{0,1},{1,2},{2,3},{3,4},{4,5},{5,6},{6,7},{7,8},{8,9},{9,10},{10,1... | collective-permute-start | bytes 786440 | tf_op jit(solution)/shard_map/ppermute | solution.py:15
  37.3 20.8 %collective-permute-start.7 = (bf16[256,4,128]{2,0,1:T(8,128)(2,1)S(1)}, bf16[256,4,128]{2,0,1:T(8,128)(2,1)S(1)}, u32[]{:S(2)}, u32[]{:S(2)}) collective-permute-start(bf16[256,4,128]{2,0,1:T(8,128)(2,1)S(1)} %add_convert_fusion.5), channel_id=1, source_target_pairs={{0,1},{1,2},{2,3},{3,4},{4,5},{5,6},{6,7},{7,8},{8,9},{9,10},{10,1... | collective-permute-start | bytes 786440 | tf_op jit(solution)/shard_map/ppermute | solution.py:15
  39.2 10.9 %collective-permute-start.3 = (bf16[256,4,128]{0,2,1:T(8,128)(2,1)S(1)}, bf16[256,4,128]{0,2,1:T(8,128)(2,1)S(1)}, u32[]{:S(2)}, u32[]{:S(2)}) collective-permute-start(bf16[256,4,128]{0,2,1:T(8,128)(2,1)S(1)} %collective-permute-done.1), channel_id=1, source_target_pairs={{0,1},{1,2},{2,3},{3,4},{4,5},{5,6},{6,7},{7,8},{8,9},{9,10},{10,1... | collective-permute-start | bytes 786440 | tf_op jit(solution)/shard_map/ppermute | solution.py:15
  43.4 6.2 %collective-permute-start.2 = (bf16[256,4,128]{2,0,1:T(8,128)(2,1)}, bf16[256,4,128]{2,0,1:T(8,128)(2,1)S(1)}, u32[]{:S(2)}, u32[]{:S(2)}) collective-permute-start(bf16[256,4,128]{2,0,1:T(8,128)(2,1)} %collective-permute-done), channel_id=1, source_target_pairs={{0,1},{1,2},{2,3},{3,4},{4,5},{5,6},{6,7},{7,8},{8,9},{9,10},{10,1... | collective-permute-start | bytes 786440 | tf_op jit(solution)/shard_map/ppermute | solution.py:15
  50.7 20.0 %copy-start.2 = (f32[256,256]{1,0:T(8,128)S(1)}, f32[256,256]{1,0:T(8,128)}, u32[]{:S(2)}) copy-start(f32[256,256]{1,0:T(8,128)} %get-tuple-element.26) | copy-start | bytes 786436
  51.0 22.2 %collective-permute-start.12 = (bf16[256,4,128]{0,2,1:T(8,128)(2,1)S(1)}, bf16[256,4,128]{0,2,1:T(8,128)(2,1)S(1)}, u32[]{:S(2)}, u32[]{:S(2)}) collective-permute-start(bf16[256,4,128]{0,2,1:T(8,128)(2,1)S(1)} %add_convert_fusion.1), channel_id=1, source_target_pairs={{0,1},{1,2},{2,3},{3,4},{4,5},{5,6},{6,7},{7,8},{8,9},{9,10},{10,1... | collective-permute-start | bytes 786440 | tf_op jit(solution)/shard_map/ppermute | solution.py:15
  58.8 26.9 %collective-permute-start.8 = (bf16[256,4,128]{2,0,1:T(8,128)(2,1)}, bf16[256,4,128]{2,0,1:T(8,128)(2,1)}, u32[]{:S(2)}, u32[]{:S(2)}) collective-permute-start(bf16[256,4,128]{2,0,1:T(8,128)(2,1)} %add_convert_fusion.4), channel_id=1, source_target_pairs={{0,1},{1,2},{2,3},{3,4},{4,5},{5,6},{6,7},{7,8},{8,9},{9,10},{10,1... | collective-permute-start | bytes 786440 | tf_op jit(solution)/shard_map/ppermute | solution.py:15
  60.7 10.5 %collective-permute-start.5 = (bf16[256,4,128]{0,2,1:T(8,128)(2,1)S(1)}, bf16[256,4,128]{0,2,1:T(8,128)(2,1)S(1)}, u32[]{:S(2)}, u32[]{:S(2)}) collective-permute-start(bf16[256,4,128]{0,2,1:T(8,128)(2,1)S(1)} %collective-permute-done.3), channel_id=1, source_target_pairs={{0,1},{1,2},{2,3},{3,4},{4,5},{5,6},{6,7},{7,8},{8,9},{9,10},{10,1... | collective-permute-start | bytes 786440 | tf_op jit(solution)/shard_map/ppermute | solution.py:15
  64.6 6.1 %collective-permute-start.4 = (bf16[256,4,128]{2,0,1:T(8,128)(2,1)S(1)}, bf16[256,4,128]{2,0,1:T(8,128)(2,1)S(1)}, u32[]{:S(2)}, u32[]{:S(2)}) collective-permute-start(bf16[256,4,128]{2,0,1:T(8,128)(2,1)S(1)} %collective-permute-done.2), channel_id=1, source_target_pairs={{0,1},{1,2},{2,3},{3,4},{4,5},{5,6},{6,7},{7,8},{8,9},{9,10},{10,1... | collective-permute-start | bytes 786440 | tf_op jit(solution)/shard_map/ppermute | solution.py:15
  70.7 0.7 copy-start.5
  72.2 23.3 %copy-start.1 = (bf16[1,256,1024]{2,1,0:T(8,128)(2,1)S(1)}, bf16[1,256,1024]{2,1,0:T(8,128)(2,1)}, u32[]{:S(2)}) copy-start(bf16[1,256,1024]{2,1,0:T(8,128)(2,1)} %param.8) | copy-start | bytes 1572868
  75.8 19.7 %collective-permute-start.13 = (bf16[256,4,128]{0,2,1:T(8,128)(2,1)}, bf16[256,4,128]{0,2,1:T(8,128)(2,1)}, u32[]{:S(2)}, u32[]{:S(2)}) collective-permute-start(bf16[256,4,128]{0,2,1:T(8,128)(2,1)} %add_convert_fusion), channel_id=1, source_target_pairs={{0,61},{1,62},{2,63},{3,0},{4,1},{5,2},{6,3},{7,4},{8,5},{9,6},{10... | collective-permute-start | bytes 786440 | tf_op jit(solution)/shard_map/ppermute | solution.py:15
  86.8 7.7 %collective-permute-start.9 = (bf16[256,4,128]{2,0,1:T(8,128)(2,1)S(1)}, bf16[256,4,128]{2,0,1:T(8,128)(2,1)S(1)}, u32[]{:S(2)}, u32[]{:S(2)}) collective-permute-start(bf16[256,4,128]{2,0,1:T(8,128)(2,1)S(1)} %add_convert_fusion.3), channel_id=1, source_target_pairs={{0,61},{1,62},{2,63},{3,0},{4,1},{5,2},{6,3},{7,4},{8,5},{9,6},{10... | collective-permute-start | bytes 786440 | tf_op jit(solution)/shard_map/ppermute | solution.py:15
where the time goes:
time: 292 us; the launch traced here: 291 us
  blocking collectives  191 us (65%)
  starting transfers between devices  51.7 us (18%)
  matrix products  23 us (8%)
  waiting for transfers between devices  10.6 us (4%)
  local copies, waits for them, and re-layouts  8.31 us (3%)
  other arithmetic  5.18 us (2%)
    psum x1, blocking collectives, body(): summed = lax.psum(terms, ('dp', 'ctx'))  191 us
    ppermute x14, starting transfers between devices, from_behind(): return lax.ppermute(value, axis, pairs)  51.7 us
    ppermute x14, waiting for transfers between devices, from_behind(): return lax.ppermute(value, axis, pairs)  10.6 us
  transfers between devices with their start and end apart: 14, of which 3 were waited for; matrix products, arithmetic and copies ran while one was open for 10% of the time, Pallas kernels for 0%

commit v1 on v0

--- a/solution.py
+++ b/solution.py
@@ -102,7 +102,7 @@
     width_rows = local.shape[1]
     share = width_rows // cycle_size
     terms = jnp.einsum("rd,rf->df", local, joined, preferred_element_type=jnp.float32)
-    summed = lax.psum(terms, ("dp", "ctx"))
+    summed = lax.psum(lax.psum(terms, "ctx"), "dp")
     mine = lax.dynamic_slice_in_dim(summed, myself * share, share, 0)
     grad_wq = mine[:, :features].astype(jnp.bfloat16)
     grad_wk = mine[:, features:].astype(jnp.bfloat16)

time: 292 us -> 807 us (2.76); the launches traced: 291 us -> 794 us
  waiting for transfers between devices: 10.6 us -> 510 us
  blocking collectives: 191 us -> 159 us
  starting transfers between devices: 51.7 us -> 78 us
  between operations: 1.85 us -> 15.3 us
    psum x0 -> x1, waiting for transfers between devices: none -> 490 us  [body(): summed = lax.psum(lax.psum(terms, 'ctx'), 'dp')]
    psum x1, blocking collectives: 191 us -> 159 us  [body(): summed = lax.psum(lax.psum(terms, 'ctx'), 'dp')]
    ppermute x14, starting transfers between devices: 51.7 us -> 78 us  [from_behind(): return lax.ppermute(value, axis, pairs)]
    ppermute x14, waiting for transfers between devices: 10.6 us -> 19.4 us  [from_behind(): return lax.ppermute(value, axis, pairs)]
  transfers between devices with their start and end apart: 14 -> 15, of which waited for: 3 -> 9; matrix products, arithmetic and copies ran while one was open for 10% -> 3% of each run, Pallas kernels for 0% -> 0%
where the time goes in v1:
time: 807 us; the launch traced here: 794 us
  waiting for transfers between devices  510 us (63%)
  blocking collectives  159 us (20%)
  starting transfers between devices  78 us (10%)
  matrix products  21.6 us (3%)
  between operations  15.3 us (2%)
    psum x1, waiting for transfers between devices, body(): summed = lax.psum(lax.psum(terms, 'ctx'), 'dp')  490 us
    psum x1, blocking collectives, body(): summed = lax.psum(lax.psum(terms, 'ctx'), 'dp')  159 us
    ppermute x14, starting transfers between devices, from_behind(): return lax.ppermute(value, axis, pairs)  78 us
    ppermute x14, waiting for transfers between devices, from_behind(): return lax.ppermute(value, axis, pairs)  19.4 us
  transfers between devices with their start and end apart: 15, of which 9 were waited for; matrix products, arithmetic and copies ran while one was open for 3% of the time, Pallas kernels for 0%

profile of v1, /device:TPU:7, one launch (start us, length us, event | category | flops | bytes accessed | tf_op | source)
XLA Modules:
  0.0 793.6 jit_solution(7418911149814118253)
XLA Ops:
  7.2 1.2 copy.87
  8.4 4.9 collective-permute-start.1
  13.4 1.5 fusion.20
  14.9 0.7 copy.157
  15.6 1.9 collective-permute-start
  18.3 1.0 select_reduce_fusion
  19.4 0.7 copy.86
  20.3 1.0 reshape_squeeze.7
  21.3 1.8 convolution_convert_fusion.3
  23.4 0.3 and_select_fusion
  23.7 1.4 multiply_convert_fusion.3
  25.1 0.5 fusion.15
  25.7 0.2 fusion.19
  25.9 4.1 collective-permute-start.10
  30.0 0.3 fusion.42
  30.4 1.5 multiply_convert_fusion.2
  31.9 0.5 fusion.14
  32.4 0.9 collective-permute-done.10
  33.3 0.2 add_convert_fusion.2
  33.6 6.8 collective-permute-start.11
  40.4 1.9 collective-permute-start.3
  42.3 3.9 collective-permute-start.2
  46.2 1.3 convolution_add_fusion.2
  47.5 2.3 collective-permute-done.2
  49.8 0.5 multiply_convert_fusion.1
  50.4 0.5 fusion.13
  50.9 0.2 convolution_bitcast_fusion.2
  51.2 6.7 collective-permute-start.12
  57.9 1.9 collective-permute-start.5
  59.9 4.1 collective-permute-start.4
  64.0 0.3 convolution_add_fusion.1
  64.3 3.0 collective-permute-done.4
  67.3 0.5 multiply_convert_fusion
  67.9 0.5 fusion.12
  68.4 0.2 convolution_bitcast_fusion.1
  68.7 11.1 %collective-permute-start.13 = (bf16[256,4,128]{0,2,1:T(8,128)(2,1)S(1)}, bf16[256,4,128]{0,2,1:T(8,128)(2,1)S(1)}, u32[]{:S(2)}, u32[]{:S(2)}) collective-permute-start(bf16[256,4,128]{0,2,1:T(8,128)(2,1)S(1)} %add_convert_fusion), channel_id=1, source_target_pairs={{0,61},{1,62},{2,63},{3,0},{4,1},{5,2},{6,3},{7,4},{8,5},{9,6},{10... | collective-permute-start | bytes 786440 | tf_op jit(solution)/shard_map/ppermute | solution.py:15
  79.9 0.3 fusion.17
  80.2 3.0 collective-permute-done.13
  83.2 2.7 convolution_bitcast_fusion
  85.9 2.1 fusion.18
  88.0 1.9 collective-permute-start.6
  90.0 1.4 fusion.44
  91.4 2.2 collective-permute-done.6
  93.6 1.3 add_convert_fusion.5
  94.9 6.9 collective-permute-start.7
  101.8 0.3 convolution_add_fusion.5
  102.1 0.3 convolution_bitcast_fusion.5
  102.5 2.6 collective-permute-done.7
  105.2 6.8 collective-permute-start.8
  112.0 0.3 convolution_add_fusion.4
  112.3 0.3 convolution_bitcast_fusion.4
  112.6 2.9 collective-permute-done.8
  115.6 0.8 add_convert_fusion.3
  116.3 14.9 %collective-permute-start.9 = (bf16[256,4,128]{2,0,1:T(8,128)(2,1)}, bf16[256,4,128]{2,0,1:T(8,128)(2,1)S(1)}, u32[]{:S(2)}, u32[]{:S(2)}) collective-permute-start(bf16[256,4,128]{2,0,1:T(8,128)(2,1)} %add_convert_fusion.3), channel_id=1, source_target_pairs={{0,61},{1,62},{2,63},{3,0},{4,1},{5,2},{6,3},{7,4},{8,5},{9,6},{10... | collective-permute-start | bytes 786440 | tf_op jit(solution)/shard_map/ppermute | solution.py:15
  131.2 0.3 fusion.16
  131.5 0.8 copy.117
  132.4 2.4 collective-permute-done.9
  134.8 0.1 copy.100
  135.0 0.8 copy.118
  135.8 490.4 %all-reduce.3.cloned.1.call-done = f32[1024,1024]{0,1:T(8,128)} async-done(((f32[1024,1024]{0,1:T(8,128)}), f32[1024,1024]{0,1:T(8,128)}) %all-reduce.3.cloned.1.call-update) | async-done | bytes 4194320 | tf_op jit(solution)/shard_map/psum | solution.py:105
  626.3 158.9 %all-reduce.4 = bf16[1024,1024]{0,1:T(8,128)(2,1)S(1)} all-reduce(f32[1024,1024]{0,1:T(8,128)} %all-reduce.3.cloned.1.call-done), channel_id=1, replica_groups=mesh['dp'=8,'ctx'=64] {'dp'}, use_global_device_ids=true, to_apply=%region_10.11 | all-reduce | flops 1048576 | bytes 6291456 | tf_op jit(solution)/shard_map/psum | solution.py:105
  785.1 0.2 dynamic-slice_convert_fusion
  785.3 0.7 copy.120
  786.0 0.7 copy.119
  (44 shorter events, 0.8 us)
Async XLA Ops:
  7.2 6.2 copy-start
  7.2 619.1 %all-reduce.3.cloned.1.call-start = ((), (), s32[]{:S(2)}) async-start(), calls=%async_computation | async-start | bytes 8388608 | tf_op jit(solution)/shard_map/psum | solution.py:105
  8.4 16.7 %copy-start.2 = (bf16[1,256,512]{1,2,0:T(8,128)(2,1)}, bf16[1,256,512]{1,2,0:T(8,128)(2,1)S(1)}, u32[]{:S(2)}) copy-start(bf16[1,256,512]{1,2,0:T(8,128)(2,1)S(1)} %copy.87) | copy-start | bytes 786436
  8.4 23.5 %collective-permute-start.1 = (bf16[256,4,128]{0,2,1:T(8,128)(2,1)S(1)}, bf16[256,4,128]{0,2,1:T(8,128)(2,1)S(1)}, u32[]{:S(2)}, u32[]{:S(2)}) collective-permute-start(bf16[256,4,128]{0,2,1:T(8,128)(2,1)S(1)} %bitcast.101), channel_id=1, source_target_pairs={{0,1},{1,2},{2,3},{3,4},{4,5},{5,6},{6,7},{7,8},{8,9},{9,10},{10,1... | collective-permute-start | bytes 786440 | tf_op jit(solution)/shard_map/ppermute | solution.py:15
  15.6 14.8 %collective-permute-start = (bf16[256,4,128]{2,0,1:T(8,128)(2,1)}, bf16[256,4,128]{2,0,1:T(8,128)(2,1)}, u32[]{:S(2)}, u32[]{:S(2)}) collective-permute-start(bf16[256,4,128]{2,0,1:T(8,128)(2,1)} %bitcast.88), channel_id=1, source_target_pairs={{0,1},{1,2},{2,3},{3,4},{4,5},{5,6},{6,7},{7,8},{8,9},{9,10},{10,1... | collective-permute-start | bytes 786440 | tf_op jit(solution)/shard_map/ppermute | solution.py:15
  25.9 7.4 collective-permute-start.10
  31.9 15.6 %copy-start.4 = (bf16[256,4,128]{0,2,1:T(8,128)(2,1)}, bf16[256,4,128]{0,2,1:T(8,128)(2,1)S(1)}, u32[]{:S(2)}) copy-start(bf16[256,4,128]{0,2,1:T(8,128)(2,1)S(1)} %collective-permute-done.1) | copy-start | bytes 786436
  33.6 17.6 %collective-permute-start.11 = (bf16[256,4,128]{0,2,1:T(8,128)(2,1)S(1)}, bf16[256,4,128]{0,2,1:T(8,128)(2,1)S(1)}, u32[]{:S(2)}, u32[]{:S(2)}) collective-permute-start(bf16[256,4,128]{0,2,1:T(8,128)(2,1)S(1)} %add_convert_fusion.2), channel_id=1, source_target_pairs={{0,1},{1,2},{2,3},{3,4},{4,5},{5,6},{6,7},{7,8},{8,9},{9,10},{10,1... | collective-permute-start | bytes 786440 | tf_op jit(solution)/shard_map/ppermute | solution.py:15
  40.4 10.0 %collective-permute-start.3 = (bf16[256,4,128]{0,2,1:T(8,128)(2,1)S(1)}, bf16[256,4,128]{0,2,1:T(8,128)(2,1)S(1)}, u32[]{:S(2)}, u32[]{:S(2)}) collective-permute-start(bf16[256,4,128]{0,2,1:T(8,128)(2,1)S(1)} %collective-permute-done.1), channel_id=1, source_target_pairs={{0,1},{1,2},{2,3},{3,4},{4,5},{5,6},{6,7},{7,8},{8,9},{9,10},{10,1... | collective-permute-start | bytes 786440 | tf_op jit(solution)/shard_map/ppermute | solution.py:15
  42.3 7.5 collective-permute-start.2
  50.4 7.6 copy-start.6
  51.2 17.4 %collective-permute-start.12 = (bf16[256,4,128]{0,2,1:T(8,128)(2,1)S(1)}, bf16[256,4,128]{0,2,1:T(8,128)(2,1)S(1)}, u32[]{:S(2)}, u32[]{:S(2)}) collective-permute-start(bf16[256,4,128]{0,2,1:T(8,128)(2,1)S(1)} %add_convert_fusion.1), channel_id=1, source_target_pairs={{0,1},{1,2},{2,3},{3,4},{4,5},{5,6},{6,7},{7,8},{8,9},{9,10},{10,1... | collective-permute-start | bytes 786440 | tf_op jit(solution)/shard_map/ppermute | solution.py:15
  57.9 9.9 %collective-permute-start.5 = (bf16[256,4,128]{0,2,1:T(8,128)(2,1)S(1)}, bf16[256,4,128]{0,2,1:T(8,128)(2,1)S(1)}, u32[]{:S(2)}, u32[]{:S(2)}) collective-permute-start(bf16[256,4,128]{0,2,1:T(8,128)(2,1)S(1)} %collective-permute-done.3), channel_id=1, source_target_pairs={{0,1},{1,2},{2,3},{3,4},{4,5},{5,6},{6,7},{7,8},{8,9},{9,10},{10,1... | collective-permute-start | bytes 786440 | tf_op jit(solution)/shard_map/ppermute | solution.py:15
  59.9 7.4 collective-permute-start.4
  67.9 0.8 copy-start.8
  67.9 15.3 %copy-start.1 = (bf16[1,256,1024]{2,1,0:T(8,128)(2,1)S(1)}, bf16[1,256,1024]{2,1,0:T(8,128)(2,1)}, u32[]{:S(2)}) copy-start(bf16[1,256,1024]{2,1,0:T(8,128)(2,1)} %param.8) | copy-start | bytes 1572868
  68.7 14.4 %collective-permute-start.13 = (bf16[256,4,128]{0,2,1:T(8,128)(2,1)S(1)}, bf16[256,4,128]{0,2,1:T(8,128)(2,1)S(1)}, u32[]{:S(2)}, u32[]{:S(2)}) collective-permute-start(bf16[256,4,128]{0,2,1:T(8,128)(2,1)S(1)} %add_convert_fusion), channel_id=1, source_target_pairs={{0,61},{1,62},{2,63},{3,0},{4,1},{5,2},{6,3},{7,4},{8,5},{9,6},{10... | collective-permute-start | bytes 786440 | tf_op jit(solution)/shard_map/ppermute | solution.py:15
  85.9 4.1 copy-start.3
  85.9 15.9 %copy-start.5 = (bf16[256,4,128]{0,2,1:T(8,128)(2,1)S(1)}, bf16[256,4,128]{0,2,1:T(8,128)(2,1)}, u32[]{:S(2)}) copy-start(bf16[256,4,128]{0,2,1:T(8,128)(2,1)} %copy-done.4) | copy-start | bytes 786436
  88.0 5.5 collective-permute-start.6
  90.0 22.0 %copy-start.7 = (bf16[256,4,128]{0,2,1:T(8,128)(2,1)S(1)}, bf16[256,4,128]{0,2,1:T(8,128)(2,1)}, u32[]{:S(2)}) copy-start(bf16[256,4,128]{0,2,1:T(8,128)(2,1)} %copy-done.6) | copy-start | bytes 786436
  94.9 36.3 %copy-start.9 = (bf16[256,4,128]{0,2,1:T(8,128)(2,1)S(1)}, bf16[256,4,128]{0,2,1:T(8,128)(2,1)}, u32[]{:S(2)}) copy-start(bf16[256,4,128]{0,2,1:T(8,128)(2,1)} %copy-done.8) | copy-start | bytes 786436
  94.9 10.2 %collective-permute-start.7 = (bf16[256,4,128]{2,0,1:T(8,128)(2,1)S(1)}, bf16[256,4,128]{2,0,1:T(8,128)(2,1)S(1)}, u32[]{:S(2)}, u32[]{:S(2)}) collective-permute-start(bf16[256,4,128]{2,0,1:T(8,128)(2,1)S(1)} %add_convert_fusion.5), channel_id=1, source_target_pairs={{0,1},{1,2},{2,3},{3,4},{4,5},{5,6},{6,7},{7,8},{8,9},{9,10},{10,1... | collective-permute-start | bytes 786440 | tf_op jit(solution)/shard_map/ppermute | solution.py:15
  105.2 10.4 %collective-permute-start.8 = (bf16[256,4,128]{2,0,1:T(8,128)(2,1)S(1)}, bf16[256,4,128]{2,0,1:T(8,128)(2,1)S(1)}, u32[]{:S(2)}, u32[]{:S(2)}) collective-permute-start(bf16[256,4,128]{2,0,1:T(8,128)(2,1)S(1)} %add_convert_fusion.4), channel_id=1, source_target_pairs={{0,1},{1,2},{2,3},{3,4},{4,5},{5,6},{6,7},{7,8},{8,9},{9,10},{10,1... | collective-permute-start | bytes 786440 | tf_op jit(solution)/shard_map/ppermute | solution.py:15
  116.3 18.5 %collective-permute-start.9 = (bf16[256,4,128]{2,0,1:T(8,128)(2,1)}, bf16[256,4,128]{2,0,1:T(8,128)(2,1)S(1)}, u32[]{:S(2)}, u32[]{:S(2)}) collective-permute-start(bf16[256,4,128]{2,0,1:T(8,128)(2,1)} %add_convert_fusion.3), channel_id=1, source_target_pairs={{0,61},{1,62},{2,63},{3,0},{4,1},{5,2},{6,3},{7,4},{8,5},{9,6},{10... | collective-permute-start | bytes 786440 | tf_op jit(solution)/shard_map/ppermute | solution.py:15
Sparse Core Ops, SparseCore 0:
  86.0 540.1 all-reduce.2
